TPU v7x, 32 devices: a whole 2x2x4 slice. The times are simulated.
32 devices in a mesh: req: 16 (over z, y, x), tp: 2 (over core).
Axes of the slice: x: 2, y: 2, z: 4, core: 2. Of those that a mesh axis runs over, the one named last changes fastest.
Arguments:
- tokens: bfloat16 [8192, 5120], P(('req', 'tp')), may hold values from -200 to 200
- norm_gain: float32 [5120], replicated, may hold values from 0.1 to 1.9
- w_query: bfloat16 [5120, 3072], P('req', 'tp'), may hold values from -0.078125 to 0.078125
- w_kv: bfloat16 [5120, 2, 1024], P('req', None, 'tp'), may hold values from -0.078125 to 0.078125
- q_gain: float32 [128], replicated, may hold values from 0.5 to 60, as said below
- k_gain: float32 [128], replicated, may hold values from 0.1 to 1.9
- seg_ids: int32 [16, 512], P('req'), may hold values from 0 to 5, never falling along the last dimension, each value on 1 to 256 neighbouring positions
- page_table: int32 [16, 8], replicated, may hold values from 0 to 127, as said below
Outputs:
- attended: bfloat16 [8192, 3072], P('req', 'tp')
- cache: bfloat16 [16, 8, 64, 2, 1024], P('req', None, None, None, 'tp')
Inputs may be any that keep to these rules, and one draw needn't show every extreme that they name: page_table[r, p] = o * 8 + s sends page p of pack r to slot s of owner o; every slot of every owner receives exactly one page, and the pages of one pack go to different owners. `seg_ids`: nondecreasing along each pack; every pack holds 6 prompts. `q_gain`: positive.
All inputs are finite; a program needn't handle non-finite values.
Results may differ from a plain program's by a relative error of at most 0.008.
The roundings to bfloat16 on the way count: a program that leaves them out, or rounds other values in their place, can miss the bound.
Values may be sent and summed in bfloat16 or wider, within the bound.
A program may use at most 128 MiB of HBM per device.

v0:
```python
import jax
import jax.numpy as jnp
from jax import lax
from jax.sharding import PartitionSpec as P

HD = 128


def rope_tables(positions, width):
    half = width // 2
    freqs = jnp.power(jnp.float32(1000000.0), -jnp.arange(half, dtype=jnp.float32) * 2.0 / width)
    angles = positions.astype(jnp.float32)[:, None] * freqs[None, :]
    angles = jnp.concatenate([angles, angles], axis=1)
    return (jnp.cos(angles), jnp.sin(angles))


def head_norm_rope(values, gain, cosine, sine):
    scaled = values * lax.rsqrt(jnp.mean(values * values, axis=-1, keepdims=True) + 1e-06) * gain
    half = values.shape[-1] // 2
    turned = jnp.concatenate([-scaled[..., half:], scaled[..., :half]], axis=-1)
    return (scaled * cosine[:, None, :] + turned * sine[:, None, :]).astype(jnp.bfloat16)


def segment_positions(seg_row):
    before = jnp.sum((seg_row[None, :] < seg_row[:, None]).astype(jnp.int32), axis=1)
    return jnp.arange(seg_row.shape[0], dtype=jnp.int32) - before


def body(tokens, norm_gain, w_query, w_kv, q_gain, k_gain, seg_ids, page_table):
    values_in = tokens.astype(jnp.float32)
    normed = (
        values_in
        * lax.rsqrt(jnp.mean(values_in * values_in, axis=1, keepdims=True) + 1e-06)
        * norm_gain
    ).astype(jnp.bfloat16)
    query_width = w_query.shape[1]
    kv_flat = w_kv.reshape(w_kv.shape[0], -1)
    whole = lax.all_gather(normed, "tp", axis=0, tiled=True)
    query = jnp.dot(
        whole,
        lax.all_gather(w_query, "req", axis=0, tiled=True),
        preferred_element_type=jnp.float32,
    )
    keyval = jnp.dot(
        whole,
        lax.all_gather(kv_flat, "req", axis=0, tiled=True),
        preferred_element_type=jnp.float32,
    )
    count = query.shape[0]
    local_heads = query_width // HD
    local_kv = kv_flat.shape[1] // (2 * HD)
    group = local_heads // local_kv
    seg_row = seg_ids[0]
    positions = segment_positions(seg_row)
    cosine, sine = rope_tables(positions, HD)
    q_normed = head_norm_rope(query.reshape(count, local_heads, HD), q_gain, cosine, sine)
    keyval = keyval.reshape(count, 2, local_kv, HD)
    k_normed = head_norm_rope(keyval[:, 0], k_gain, cosine, sine)
    v_round = keyval[:, 1].astype(jnp.bfloat16)
    pages_dev = page_table.shape[1]
    page_len = count // pages_dev
    devices = lax.axis_size("req")
    me = lax.axis_index("req")
    stacked = jnp.stack([k_normed, v_round], axis=1).reshape(
        pages_dev, page_len * 2 * local_kv * HD
    )
    my_row = lax.dynamic_slice_in_dim(page_table, me, 1, 0)[0]
    owners = my_row // pages_dev
    send_map = (owners[None, :] == jnp.arange(devices, dtype=jnp.int32)[:, None]).astype(
        jnp.bfloat16
    )
    outgoing = jnp.dot(send_map, stacked, preferred_element_type=jnp.float32).astype(jnp.bfloat16)
    incoming = lax.all_to_all(outgoing, "req", split_axis=0, concat_axis=0, tiled=True)
    targets = me * pages_dev + jnp.arange(pages_dev, dtype=jnp.int32)
    recv_map = jnp.any(page_table[None, :, :] == targets[:, None, None], axis=2).astype(
        jnp.bfloat16
    )
    cache = jnp.dot(recv_map, incoming, preferred_element_type=jnp.float32).astype(jnp.bfloat16)
    cache = cache.reshape(1, pages_dev, page_len, 2, local_kv * HD)
    grouped_q = q_normed.reshape(count, local_kv, group, HD)
    scale = HD ** (-0.5)
    index = jnp.arange(count, dtype=jnp.int32)
    scores = (
        jnp.einsum("qcgd,kcd->cgqk", grouped_q, k_normed, preferred_element_type=jnp.float32)
        * scale
    )
    allowed = (seg_row[:, None] == seg_row[None, :]) & (index[None, :] <= index[:, None])
    scores = jnp.where(allowed[None, None], scores, -1e30)
    probs = jax.nn.softmax(scores, axis=-1).astype(jnp.bfloat16)
    attended = jnp.einsum("cgqk,kcd->qcgd", probs, v_round, preferred_element_type=jnp.float32)
    attended = attended.reshape(count, local_heads * HD).astype(jnp.bfloat16)
    return (attended, cache)


def solution(mesh):
    placed = (
        P(("req", "tp"), None),
        P(),
        P("req", "tp"),
        P("req", None, "tp"),
        P(),
        P(),
        P("req", None),
        P(),
    )
    return jax.shard_map(
        body,
        mesh=mesh,
        in_specs=placed,
        out_specs=(P("req", "tp"), P("req", None, None, None, "tp")),
        check_vma=False,
    )
```

profile of v0, /device:TPU:0, one launch (start us, length us, event | category | flops | bytes accessed | tf_op | source)
XLA Modules:
  0.0 427.6 jit_solution(11398124974364142847)
XLA Ops:
  7.2 0.0 all-gather.4.cloned.1.call-start
  7.2 2.5 fusion.7
  9.7 3.0 fusion.9
  12.8 0.0 all-gather.6.cloned.1.call-start
  12.9 0.9 copy.78
  13.8 0.0 all-gather.8.cloned.1.call-start
  13.9 0.7 all-gather.8.cloned.1.call-update
  14.6 0.2 fusion.36
  14.8 0.2 convert_reduce_fusion
  15.0 0.1 broadcast_multiply_fusion
  15.1 1.0 fusion.34
  16.1 14.8 %all-gather.4.cloned.1.call-done = bf16[512,5120]{1,0:T(8,128)(2,1)} async-done(((bf16[256,5120]{1,0:T(8,128)(2,1)}), bf16[512,5120]{1,0:T(8,128)(2,1)}) %all-gather.4.cloned.1.call-update) | async-done | bytes 5242896 | tf_op jit(solution)/shard_map/all_gather | solution.py:38
  30.9 135.9 %all-gather.6.cloned.1.call-done = bf16[5120,1024]{1,0:T(8,128)(2,1)} async-done(((bf16[320,1024]{1,0:T(8,128)(2,1)}), bf16[5120,1024]{1,0:T(8,128)(2,1)}) %all-gather.6.cloned.1.call-update) | async-done | bytes 10485776 | tf_op jit(solution)/shard_map/all_gather | solution.py:46
  166.8 9.9 %fusion.45 = f32[512,1024]{0,1:T(8,128)S(1)} fusion(bf16[512,5120]{1,0:T(8,128)(2,1)} %all-gather.4.cloned.1.call-done, bf16[5120,1024]{1,0:T(8,128)(2,1)} %all-gather.6.cloned.1.call-done), kind=kOutput, calls=%fused_computation.79 | convolution fusion | flops 5368709120 | bytes 17825792 | tf_op jit(solution)/shard_map/reshape | solution.py:57
  176.8 0.1 slice.39
  176.8 0.1 fusion.25
  177.0 0.2 fusion.26
  177.2 1.2 copy-done
  178.4 1.2 fusion.42
  179.6 0.4 fusion.24
  180.0 0.1 pad_maximum_fusion
  180.1 0.8 copy.65
  180.9 0.8 reshape.211
  181.7 0.7 fusion.1
  182.4 0.5 broadcast.139
  182.9 2.9 reduce.2
  185.8 4.0 reshape.216
  189.8 3.9 all-to-all-start
  193.8 0.1 compare_reduce_fusion
  193.9 0.9 fusion.27
  194.8 64.4 %all-to-all-done = bf16[16,2,32768]{2,1,0:T(2,128)(2,1)S(1)} async-done(((bf16[16,2,32768]{2,1,0:T(2,128)(2,1)}), bf16[16,2,32768]{2,1,0:T(2,128)(2,1)S(1)}, u32[]{:S(2)}, u32[]{:S(2)}) %all-to-all-start) | async-done | bytes 2097184 | tf_op jit(solution)/shard_map/all_to_all | solution.py:73
  259.2 6.8 %reshape.217 = bf16[16,1,65536]{2,1,0:T(2,128)(2,1)} reshape(bf16[16,2,32768]{2,1,0:T(2,128)(2,1)S(1)} %all-to-all-done) | data formatting | bytes 4194304
  265.9 4.5 %convolution_convert_fusion.1 = bf16[8,65536]{1,0:T(8,128)(2,1)S(1)} fusion(pred[8,16]{1,0:T(8,128)(4,1)S(1)} %compare_reduce_fusion, bf16[16,1,65536]{2,1,0:T(2,128)(2,1)} %reshape.217), kind=kOutput, calls=%fused_computation.3 | convolution fusion | flops 17301504 | bytes 3145856 | tf_op jit(solution)/shard_map/dot_general | solution.py:78
  270.5 1.8 copy.68
  272.2 113.4 %all-gather.8.cloned.1.call-done = bf16[5120,1536]{1,0:T(8,128)(2,1)} async-done(((bf16[320,1536]{1,0:T(8,128)(2,1)}), bf16[5120,1536]{1,0:T(8,128)(2,1)}) %all-gather.8.cloned.1.call-update) | async-done | bytes 15728656 | tf_op jit(solution)/shard_map/all_gather | solution.py:41
  385.7 12.9 %fusion.46 = f32[512,1536]{0,1:T(8,128)S(1)} fusion(bf16[512,5120]{1,0:T(8,128)(2,1)} %all-gather.4.cloned.1.call-done, bf16[5120,1536]{1,0:T(8,128)(2,1)} %all-gather.8.cloned.1.call-done), kind=kOutput, calls=%fused_computation.80 | convolution fusion | flops 8053063680 | bytes 24117248 | tf_op jit(solution)/shard_map/dot_general | solution.py:39
  398.5 0.4 multiply_reduce_fusion
  399.0 0.2 copy-done.12
  399.2 0.6 multiply_multiply_fusion
  399.8 0.4 slice_negate_fusion
  400.2 0.8 copy-done.1
  401.0 0.0 copy-done.4
  401.1 0.2 copy-done.7
  401.2 0.2 copy-done.8
  401.4 2.1 fusion.15
  403.5 10.4 %fusion.43 = (f32[4,3,512]{2,1,0:T(4,128)S(1)}, f32[4,3,512,512]{2,3,1,0:T(8,128)}) fusion(f32[4,512,512,3]{2,1,3,0:T(8,128)S(1)} %fusion.15, pred[512,512]{0,1:T(8,128)(4,1)} %fusion.27), kind=kOutput, calls=%fused_computation.77 | output fusion | flops 18874880 | bytes 25452544 | tf_op jit(solution)/shard_map/sub | solution.py:89
  413.9 5.7 %fusion.14 = bf16[4,128,3,512]{3,1,2,0:T(8,128)(2,1)S(1)} fusion(f32[4,3,512,512]{2,3,1,0:T(8,128)} %get-tuple-element.21, f32[4,3,512]{2,1,0:T(4,128)S(1)} %get-tuple-element.20, f32[512,2,4,128]{0,3,2,1:T(8,128)S(1)} %bitcast.65), kind=kOutput, calls=%fused_computation.24 | convolution fusion | flops 812384256 | bytes 14712832 | tf_op jit(solution)/shard_map/cgqk,kcd->qcgd/dot_general | solution.py:90
  419.5 1.6 copy.67
  (31 shorter events, 0.2 us)
Async XLA Ops:
  7.2 2.6 copy-start.2
  7.2 23.7 %all-gather.4.cloned.1.call-start = ((), (), s32[]{:S(2)}) async-start(), calls=%async_computation.1 | async-start | bytes 7864320 | tf_op jit(solution)/shard_map/all_gather | solution.py:38
  9.7 3.1 copy-start.9
  12.8 1.8 copy-start.11
  12.8 2.0 copy-start.10
  12.8 154.0 %all-gather.6.cloned.1.call-start = ((), (), s32[]{:S(2)}) async-start(), calls=%async_computation.2 | async-start | bytes 11141120 | tf_op jit(solution)/shard_map/all_gather | solution.py:46
  13.8 371.8 %all-gather.8.cloned.1.call-start = ((), (), s32[]{:S(2)}) async-start(), calls=%async_computation.3 | async-start | bytes 16711680 | tf_op jit(solution)/shard_map/all_gather | solution.py:41
  16.0 163.6 %copy-start.3 = (f32[512,128]{0,1:T(8,128)}, f32[512,128]{0,1:T(8,128)S(1)}, u32[]{:S(2)}) copy-start(f32[512,128]{0,1:T(8,128)S(1)} %get-tuple-element.19) | copy-start | bytes 786436
  16.1 160.9 %copy-start.13 = (f32[128]{0:T(128)S(1)}, f32[128]{0:T(128)}, u32[]{:S(2)}) copy-start(f32[128]{0:T(128)} %param.13) | copy-start | bytes 1540
  176.8 2.8 copy-start.5
  177.2 1.2 copy-start
  189.8 69.4 %all-to-all-start = ((bf16[16,2,32768]{2,1,0:T(2,128)(2,1)}), bf16[16,2,32768]{2,1,0:T(2,128)(2,1)S(1)}, u32[]{:S(2)}, u32[]{:S(2)}) async-start(bf16[16,2,32768]{2,1,0:T(2,128)(2,1)} %reshape.216), calls=%async_computation | async-start | bytes 4194304 | tf_op jit(solution)/shard_map/all_to_all | solution.py:73
  398.5 0.7 copy-start.12
  399.8 1.2 copy-start.1
  399.8 1.3 copy-start.4
  399.8 1.4 copy-start.7
  399.8 1.6 copy-start.8
  403.5 10.4 %copy-start.6 = (f32[512,1024]{0,1:T(8,128)S(1)}, f32[512,1024]{0,1:T(8,128)}, u32[]{:S(2)}) copy-start(f32[512,1024]{0,1:T(8,128)} %copy-done.5) | copy-start | bytes 6291460
Sparse Core Ops, SparseCore 0:
  12.9 17.9 all-gather.3
  34.2 132.6 all-gather.5
  169.6 215.9 all-gather.7
where the time goes:
time: 428 us
  waiting for transfers between devices  329 us (77%)
  matrix products  35.7 us (8%)
  other arithmetic  24.7 us (6%)
  local copies, waits for them, and re-layouts  19.8 us (5%)
  between operations  14.1 us (3%)
    all_gather x1, waiting for transfers between devices, body(): lax.all_gather(kv_flat, 'req', axis=0, tiled=True)  136 us
    all_gather x1, waiting for transfers between devices, body(): lax.all_gather(w_query, 'req', axis=0, tiled=True)  113 us
    all_to_all x1, waiting for transfers between devices, body(): lax.all_to_all(outgoing, 'req', split_axis=0, concat_axis=0, tiled=True)  64.4 us
    unnamed x33, local copies, waits for them, and re-layouts  17.7 us
    all_gather x1, waiting for transfers between devices, body(): whole = lax.all_gather(normed, 'tp', axis=0, tiled=True)  14.8 us
    dot_general x1, matrix products, body(): jnp.dot(whole, lax.all_gather(w_query, 'req', axis=0, tiled=True), prefer...  12.9 us
    sub x1, other arithmetic, body(): probs = jax.nn.softmax(scores, axis=-1).astype(jnp.bfloat16)  10.4 us
    reshape x1, matrix products, body(): keyval = keyval.reshape(count, 2, local_kv, HD)  9.91 us
  transfers between devices with their start and end apart: 4, of which 4 were waited for; matrix products, arithmetic and copies ran while one was open for 9% of the time, Pallas kernels for 0%

commit v1 on v0

--- a/solution.py
+++ b/solution.py
@@ -1,6 +1,10 @@
+import functools
+
 import jax
 import jax.numpy as jnp
 from jax import lax
+from jax.experimental import pallas as pl
+from jax.experimental.pallas import tpu as pltpu
 from jax.sharding import PartitionSpec as P
 
 HD = 128
@@ -92,6 +96,409 @@
     return (attended, cache)
 
 
+MESH = pl.DeviceIdType.MESH
+SIDE = 2
+PLANE = SIDE * SIDE
+PARTS = 4
+
+
+def place():
+    me = lax.axis_index("req")
+    core = lax.axis_index("tp")
+    z = me // PLANE
+    q = me % PLANE
+    across = q + 1 - 2 * (q % SIDE)
+    along = (q + SIDE) % PLANE
+    diagonal = PLANE - 1 - q
+    return me, core, z, q, across, along, diagonal
+
+
+def gather_kernel(depth, x_ref, w_ref, seg_ref, xs_ref, ws_ref, segs_ref,
+                  xbuf, wbuf, sbuf, own_sem, w_send, w_recv, up_send, up_recv, down_send, down_recv,
+                  x_send, x_recv, hop_send, hop_recv, near_send, near_recv, s_send, s_recv):
+    me, core, z, q, across, along, diagonal = place()
+    base = z * PLANE
+    mates = (across, along, diagonal)
+    barrier = pltpu.get_barrier_semaphore()
+    for mate in mates:
+        pl.semaphore_signal(barrier, inc=1, device_id=(base + mate, core), device_id_type=MESH)
+    pl.semaphore_signal(barrier, inc=1, device_id=(me, 1 - core), device_id_type=MESH)
+
+    @pl.when(z > 0)
+    def _():
+        pl.semaphore_signal(barrier, inc=1, device_id=(me - PLANE, core), device_id_type=MESH)
+
+    @pl.when(z < depth - 1)
+    def _():
+        pl.semaphore_signal(barrier, inc=1, device_id=(me + PLANE, core), device_id_type=MESH)
+
+    load_w = pltpu.make_async_copy(w_ref.at[q], wbuf, own_sem.at[0])
+    load_x = pltpu.make_async_copy(x_ref, xbuf, own_sem.at[1])
+    load_s = pltpu.make_async_copy(seg_ref, sbuf, own_sem.at[2])
+    load_w.start()
+    load_x.start()
+    load_s.start()
+    pl.semaphore_wait(barrier, len(mates) + 1 + (z > 0).astype(jnp.int32) + (z < depth - 1).astype(jnp.int32))
+    rows = x_ref.shape[0] // PARTS
+
+    def remote(source, target, send, receive, device):
+        return pltpu.make_async_remote_copy(
+            src_ref=source, dst_ref=target, send_sem=send, recv_sem=receive,
+            device_id=device, device_id_type=MESH)
+
+    def w_out(i):
+        return remote(w_ref.at[mates[i]], ws_ref.at[z, q], w_send.at[i], w_recv.at[i], (base + mates[i], core))
+
+    def w_in(i):
+        return remote(w_ref.at[mates[i]], ws_ref.at[z, mates[i]], w_send.at[i], w_recv.at[i], (base + mates[i], core))
+
+    def up(d, i, order):
+        block = ws_ref.at[jnp.maximum(z - d, 0), order[i]]
+        return remote(block, block, up_send.at[d, i], up_recv.at[d, i], (jnp.minimum(me + PLANE, depth * PLANE - 1), core))
+
+    def down(d, i, order):
+        block = ws_ref.at[jnp.minimum(z + d, depth - 1), order[i]]
+        return remote(block, block, down_send.at[d, i], down_recv.at[d, i], (jnp.maximum(me - PLANE, 0), core))
+
+    order = (q,) + mates
+
+    def piece(owner, lane, k):
+        return xs_ref.at[owner, lane, pl.ds(k * rows, rows)]
+
+    def x_out(i, k):
+        return remote(x_ref.at[pl.ds(k * rows, rows)], piece(q, core, k), x_send.at[i, k], x_recv.at[i, k], (base + mates[i], core))
+
+    def x_in(i, k):
+        return remote(x_ref.at[pl.ds(k * rows, rows)], piece(mates[i], core, k), x_send.at[i, k], x_recv.at[i, k], (base + mates[i], core))
+
+    def hop(owner, k, target):
+        return remote(piece(owner, core, k), piece(owner, core, k), hop_send.at[k], hop_recv.at[k], (base + target, core))
+
+    def near(i, k):
+        source = x_ref.at[pl.ds(k * rows, rows)] if i == 0 else piece(order[i], core, k)
+        return remote(source, piece(order[i], core, k), near_send.at[i, k], near_recv.at[i, k], (me, 1 - core))
+
+    def near_in(i, k):
+        block = piece(order[i], 1 - core, k)
+        return remote(block, block, near_send.at[i, k], near_recv.at[i, k], (me, 1 - core))
+
+    def s_out(i):
+        return remote(seg_ref, segs_ref.at[q], s_send.at[i], s_recv.at[i], (base + mates[i], core))
+
+    def s_in(i):
+        return remote(seg_ref, segs_ref.at[mates[i]], s_send.at[i], s_recv.at[i], (base + mates[i], core))
+
+    for i in (2, 0, 1):
+        w_out(i).start()
+    for i in range(3):
+        s_out(i).start()
+    for k in range(PARTS):
+        x_out(0, k).start()
+        x_out(1, k).start()
+    load_w.wait()
+    save_w = pltpu.make_async_copy(wbuf, ws_ref.at[z, q], own_sem.at[0])
+    save_w.start()
+    load_s.wait()
+    save_s = pltpu.make_async_copy(sbuf, segs_ref.at[q], own_sem.at[2])
+    save_s.start()
+    load_x.wait()
+    save_x = pltpu.make_async_copy(xbuf, xs_ref.at[q, core], own_sem.at[1])
+    save_x.start()
+    save_w.wait()
+
+    def push(d, i):
+        @pl.when((z < depth - 1) & (z >= d))
+        def _():
+            up(d, i, order).start()
+
+        @pl.when((z > 0) & (z + d < depth))
+        def _():
+            down(d, i, order).start()
+
+    def arrive_up(d, i):
+        block = ws_ref.at[jnp.maximum(z - d, 0), order[i]]
+        remote(block, block, up_send.at[d - 1, i], up_recv.at[d - 1, i], (jnp.maximum(me - PLANE, 0), core)).wait_recv()
+
+    def arrive_down(d, i):
+        block = ws_ref.at[jnp.minimum(z + d, depth - 1), order[i]]
+        remote(block, block, down_send.at[d - 1, i], down_recv.at[d - 1, i], (jnp.minimum(me + PLANE, depth * PLANE - 1), core)).wait_recv()
+
+    def advance(d, i):
+        @pl.when(z >= d)
+        def _():
+            arrive_up(d, i)
+            if d < depth - 1:
+                @pl.when(z < depth - 1)
+                def _():
+                    up(d, i, order).start()
+
+        @pl.when(z + d < depth)
+        def _():
+            arrive_down(d, i)
+            if d < depth - 1:
+                @pl.when(z > 0)
+                def _():
+                    down(d, i, order).start()
+
+    push(0, 0)
+    for k in range(PARTS):
+        near(0, k).start()
+    for i in (0, 1, 2):
+        w_in(i).wait_recv()
+        push(0, i + 1)
+    for k in range(PARTS):
+        x_in(0, k).wait_recv()
+
+        @pl.when(core == 0)
+        def _():
+            hop(across, k, along).start()
+
+        near(1, k).start()
+        x_in(1, k).wait_recv()
+
+        @pl.when(core == 1)
+        def _():
+            hop(along, k, across).start()
+
+        near(2, k).start()
+        advance(1, k)
+    for k in range(PARTS):
+        advance(2, k)
+        hop(diagonal, k, along).wait_recv()
+        near(3, k).start()
+    for i in range(PLANE):
+        for d in range(3, depth):
+            advance(d, i)
+    for k in range(PARTS):
+        for i in range(PLANE):
+            near_in(i, k).wait_recv()
+    for i in range(3):
+        s_in(i).wait_recv()
+        s_out(i).wait_send()
+        w_out(i).wait_send()
+    for k in range(PARTS):
+        x_out(0, k).wait_send()
+        x_out(1, k).wait_send()
+        hop(across, k, along).wait_send()
+        for i in range(PLANE):
+            near(i, k).wait_send()
+    for d in range(depth - 1):
+        for i in range(PLANE):
+            @pl.when((z < depth - 1) & (z >= d))
+            def _():
+                up(d, i, order).wait_send()
+
+            @pl.when((z > 0) & (z + d < depth))
+            def _():
+                down(d, i, order).wait_send()
+    save_x.wait()
+    save_s.wait()
+
+
+def gather(normed, blocks, seg, depth):
+    rows, width = normed.shape
+    dma = pltpu.SemaphoreType.DMA
+    return pl.pallas_call(
+        functools.partial(gather_kernel, depth),
+        out_shape=(
+            jax.ShapeDtypeStruct((PLANE, 2, rows, width), normed.dtype),
+            jax.ShapeDtypeStruct((depth,) + blocks.shape, blocks.dtype),
+            jax.ShapeDtypeStruct((PLANE,) + seg.shape, seg.dtype),
+        ),
+        in_specs=[pl.BlockSpec(memory_space=pl.ANY)] * 3,
+        out_specs=(pl.BlockSpec(memory_space=pl.ANY),) * 3,
+        scratch_shapes=[
+            pltpu.VMEM(normed.shape, normed.dtype),
+            pltpu.VMEM(blocks.shape[1:], blocks.dtype),
+            pltpu.VMEM(seg.shape, seg.dtype),
+            dma((3,)), dma((3,)), dma((3,)),
+            dma((depth - 1, PLANE)), dma((depth - 1, PLANE)), dma((depth - 1, PLANE)), dma((depth - 1, PLANE)),
+            dma((2, PARTS)), dma((2, PARTS)), dma((PARTS,)), dma((PARTS,)),
+            dma((PLANE, PARTS)), dma((PLANE, PARTS)), dma((3,)), dma((3,)),
+        ],
+        compiler_params=pltpu.CompilerParams(collective_id=0, has_side_effects=True),
+    )(normed, blocks, seg)
+
+
+def return_kernel(total, att_ref, page_ref, out_ref, in_ref, abuf, pbuf, own_sem, a_send, a_recv, p_send, p_recv):
+    me, core, z, q, across, along, diagonal = place()
+    base = z * PLANE
+    mates = (across, along, diagonal)
+    barrier = pltpu.get_barrier_semaphore()
+    for d in range(1, total):
+        pl.semaphore_signal(barrier, inc=1, device_id=((me + d) % total, core), device_id_type=MESH)
+    load_a = pltpu.make_async_copy(att_ref.at[q], abuf, own_sem.at[0])
+    load_p = pltpu.make_async_copy(page_ref.at[me], pbuf, own_sem.at[1])
+    load_a.start()
+    load_p.start()
+    pl.semaphore_wait(barrier, total - 1)
+    width = att_ref.shape[2]
+
+    def columns(owner):
+        return out_ref.at[:, pl.ds(pl.multiple_of(owner * width, 128), width)]
+
+    def a_copy(i, owner):
+        return pltpu.make_async_remote_copy(
+            src_ref=att_ref.at[mates[i]], dst_ref=columns(owner), send_sem=a_send.at[i], recv_sem=a_recv.at[i],
+            device_id=(base + mates[i], core), device_id_type=MESH)
+
+    def p_copy(d, slot, target):
+        return pltpu.make_async_remote_copy(
+            src_ref=page_ref.at[target], dst_ref=in_ref.at[slot], send_sem=p_send.at[d - 1], recv_sem=p_recv.at[d - 1],
+            device_id=(target, core), device_id_type=MESH)
+
+    far = [d for d in range(1, total)]
+    for d in far:
+        p_copy(d, me, (me + d) % total).start()
+    for i in (2, 0, 1):
+        a_copy(i, q).start()
+    load_a.wait()
+    load_p.wait()
+    save_a = pltpu.make_async_copy(abuf, columns(q), own_sem.at[0])
+    save_p = pltpu.make_async_copy(pbuf, in_ref.at[me], own_sem.at[1])
+    save_a.start()
+    save_p.start()
+    for i in range(3):
+        a_copy(i, mates[i]).wait_recv()
+        a_copy(i, q).wait_send()
+    for d in far:
+        p_copy(d, (me + total - d) % total, (me + d) % total).wait_recv()
+        p_copy(d, me, (me + d) % total).wait_send()
+    save_a.wait()
+    save_p.wait()
+
+
+def give_back(attended, pages):
+    total = pages.shape[0]
+    dma = pltpu.SemaphoreType.DMA
+    packs, count, width = attended.shape
+    return pl.pallas_call(
+        functools.partial(return_kernel, total),
+        out_shape=(
+            jax.ShapeDtypeStruct((count, packs * width), attended.dtype),
+            jax.ShapeDtypeStruct(pages.shape, pages.dtype),
+        ),
+        in_specs=[pl.BlockSpec(memory_space=pl.ANY)] * 2,
+        out_specs=(pl.BlockSpec(memory_space=pl.ANY),) * 2,
+        scratch_shapes=[
+            pltpu.VMEM(attended.shape[1:], attended.dtype),
+            pltpu.VMEM(pages.shape[1:], pages.dtype),
+            dma((2,)), dma((3,)), dma((3,)), dma((total - 1,)), dma((total - 1,)),
+        ],
+        compiler_params=pltpu.CompilerParams(collective_id=1, has_side_effects=True),
+    )(attended, pages)
+
+
+def pick_kernel(index_ref, kv_ref, out_ref):
+    owners, packs = out_ref.shape[0], out_ref.shape[1]
+
+    def one(step, carry):
+        o, p = step // packs, step % packs
+        out_ref[o, p] = kv_ref[p, index_ref[o, p]]
+        return carry
+
+    lax.fori_loop(0, owners * packs, one, 0)
+
+
+def pick_pages(index, kv):
+    packs, pages, rows, width = kv.shape
+    return pl.pallas_call(
+        pick_kernel,
+        out_shape=jax.ShapeDtypeStruct((index.shape[0], packs, rows, width), kv.dtype),
+        in_specs=[pl.BlockSpec(memory_space=pltpu.SMEM), pl.BlockSpec(memory_space=pltpu.VMEM)],
+        out_specs=pl.BlockSpec(memory_space=pltpu.VMEM),
+    )(index, kv)
+
+
+def plane_body(tokens, norm_gain, w_query, w_kv, q_gain, k_gain, seg_ids, page_table):
+    me = lax.axis_index("req")
+    devices = lax.axis_size("req")
+    depth = devices // PLANE
+    z = me // PLANE
+    values_in = tokens.astype(jnp.float32)
+    normed = (
+        values_in
+        * lax.rsqrt(jnp.mean(values_in * values_in, axis=1, keepdims=True) + 1e-06)
+        * norm_gain
+    ).astype(jnp.bfloat16)
+    inner = w_query.shape[0]
+    q_width = w_query.shape[1] // PLANE
+    group = q_width // HD
+    blocks = jnp.concatenate(
+        [
+            w_query.reshape(inner, PLANE, q_width),
+            w_kv[:, 0].reshape(inner, PLANE, HD),
+            w_kv[:, 1].reshape(inner, PLANE, HD),
+        ],
+        axis=2,
+    ).transpose(1, 0, 2)
+    count = seg_ids.shape[1]
+    xs, ws, segs = gather(normed, blocks, seg_ids.reshape(-1, HD), depth)
+    everything = jnp.dot(
+        xs.reshape(PLANE * count, -1),
+        ws.reshape(devices * inner, -1),
+        preferred_element_type=jnp.float32,
+    )
+    seg = segs.reshape(PLANE, count)
+    positions = jax.vmap(segment_positions)(seg)
+    cosine, sine = rope_tables(positions.reshape(-1), HD)
+    q_normed = head_norm_rope(everything[:, :q_width].reshape(-1, group, HD), q_gain, cosine, sine)
+    k_normed = head_norm_rope(everything[:, None, q_width : q_width + HD], k_gain, cosine, sine)[:, 0]
+    v_round = everything[:, q_width + HD :].astype(jnp.bfloat16)
+    pages_dev = page_table.shape[1]
+    page_len = count // pages_dev
+    kv = jnp.concatenate([k_normed, v_round], axis=1).reshape(PLANE, pages_dev, page_len, 2 * HD)
+    rows = lax.dynamic_slice_in_dim(page_table, z * PLANE, PLANE, 0) // pages_dev
+    match = rows[None, :, :] == jnp.arange(devices, dtype=jnp.int32)[:, None, None]
+    index = jnp.sum(match * jnp.arange(pages_dev, dtype=jnp.int32), axis=2)
+    outgoing = pick_pages(index, kv)
+    scale = HD ** (-0.5)
+    order = jnp.arange(count, dtype=jnp.int32)
+    scores = (
+        jnp.einsum(
+            "pqgd,pkd->pgqk",
+            q_normed.reshape(PLANE, count, group, HD),
+            k_normed.reshape(PLANE, count, HD),
+            preferred_element_type=jnp.float32,
+        )
+        * scale
+    )
+    allowed = (seg[:, :, None] == seg[:, None, :]) & (order[None, None, :] <= order[None, :, None])
+    scores = jnp.where(allowed[:, None], scores, -1e30)
+    probs = jax.nn.softmax(scores, axis=-1).astype(jnp.bfloat16)
+    attended = jnp.einsum(
+        "pgqk,pkd->pqgd", probs, v_round.reshape(PLANE, count, HD), preferred_element_type=jnp.float32
+    )
+    attended = attended.reshape(PLANE, count, q_width).astype(jnp.bfloat16)
+    attended, incoming = give_back(attended, outgoing)
+    targets = me * pages_dev + jnp.arange(pages_dev, dtype=jnp.int32)
+    found = jnp.any(page_table[None, :, :] == targets[:, None, None], axis=2)
+    source = jnp.sum(found * jnp.arange(devices, dtype=jnp.int32), axis=1)
+    cache = collect(source, incoming)
+    return (attended, cache[None])
+
+
+def collect_kernel(source_ref, in_ref, out_ref):
+    slots = out_ref.shape[0]
+    for s in range(slots):
+        r = source_ref[s]
+        for h in range(PLANE):
+            page = in_ref[(r // PLANE) * PLANE + h, r % PLANE]
+            for half in range(2):
+                out_ref[s, :, half, h * HD : (h + 1) * HD] = page[:, half * HD : (half + 1) * HD]
+
+
+def collect(source, incoming):
+    slots = source.shape[0]
+    rows = incoming.shape[2]
+    return pl.pallas_call(
+        collect_kernel,
+        out_shape=jax.ShapeDtypeStruct((slots, rows, 2, PLANE * HD), incoming.dtype),
+        in_specs=[pl.BlockSpec(memory_space=pltpu.SMEM), pl.BlockSpec(memory_space=pltpu.VMEM)],
+        out_specs=pl.BlockSpec(memory_space=pltpu.VMEM),
+    )(source, incoming)
+
+
 def solution(mesh):
     placed = (
         P(("req", "tp"), None),
@@ -103,8 +510,9 @@
         P("req", None),
         P(),
     )
+    planes = mesh.shape["req"] == 4 * PLANE and mesh.shape["tp"] == 2
     return jax.shard_map(
-        body,
+        plane_body if planes else body,
         mesh=mesh,
         in_specs=placed,
         out_specs=(P("req", "tp"), P("req", None, None, None, "tp")),

time: 428 us -> 281 us (0.66)
  waiting for transfers between devices: 329 us -> 0 us
  Pallas kernels: 0 us -> 184 us
  other arithmetic: 24.7 us -> 40.6 us
  between operations: 14.1 us -> 1.01 us
  matrix products: 35.7 us -> 28.2 us
  local copies, waits for them, and re-layouts: 19.8 us -> 26.5 us
    all_gather x3 -> x0, waiting for transfers between devices: 264 us -> none  [the longest x1 136 us: body(): lax.all_gather(kv_flat, 'req', axis=0, tiled=True)]
    pallas_call x0 -> x4, Pallas kernels: none -> 184 us  [the longest x1 126 us: gather(): pl.pallas_call(functools.partial(gather_kernel, depth), out_shape=(jax.Sh...]
    all_to_all x1 -> x0, waiting for transfers between devices: 64.4 us -> none  [body(): lax.all_to_all(outgoing, 'req', split_axis=0, concat_axis=0, tiled=True)]
    unnamed x33 -> x31, local copies, waits for them, and re-layouts: 17.7 us -> 4.53 us
    reshape x1 -> x0, matrix products: 9.91 us -> none  [body(): keyval = keyval.reshape(count, 2, local_kv, HD)]
    slice x1 -> x4, local copies, waits for them, and re-layouts: 0.07 us -> 9.72 us  [the longest x2 4.24 us: plane_body(): everything[:, :q_width].reshape(-1, group, HD)]
    convert_element_type x1 -> x2, other arithmetic: 0.41 us -> 8.31 us  [head_norm_rope(): (scaled * cosine[:, None, :] + turned * sine[:, None, :]).astype(jnp.bflo...]
    cos x1, other arithmetic: 0.97 us -> 8.38 us  [rope_tables(): return (jnp.cos(angles), jnp.sin(angles))]
  transfers between devices with their start and end apart: 4 -> 0, of which waited for: 4 -> 0; matrix products, arithmetic and copies ran while one was open for 9% -> 0% of each run, Pallas kernels for 0% -> 0%
where the time goes in v1:
time: 281 us; the launch traced here: 280 us
  Pallas kernels  184 us (65%)
  other arithmetic  40.6 us (14%)
  matrix products  28.2 us (10%)
  local copies, waits for them, and re-layouts  26.5 us (9%)
    pallas_call x1, Pallas kernels, gather(): pl.pallas_call(functools.partial(gather_kernel, depth), out_shape=(jax.Sh...  126 us
    pallas_call x1, Pallas kernels, give_back(): pl.pallas_call(functools.partial(return_kernel, total), out_shape=(jax.Sh...  48.9 us
    dot_general x1, matrix products, plane_body(): jnp.dot(xs.reshape(PLANE * count, -1), ws.reshape(devices * inner, -1), p...  20.7 us
    sub x1, other arithmetic, plane_body(): probs = jax.nn.softmax(scores, axis=-1).astype(jnp.bfloat16)  10.9 us
    cos x1, other arithmetic, rope_tables(): return (jnp.cos(angles), jnp.sin(angles))  8.38 us
    convert_element_type x2, other arithmetic, head_norm_rope(): (scaled * cosine[:, None, :] + turned * sine[:, None, :]).astype(jnp.bflo...  8.31 us
    concatenate x2, local copies, waits for them, and re-layouts, head_norm_rope(): turned = jnp.concatenate([-scaled[..., half:], scaled[..., :half]], axis=-1)  6.28 us
    dot_general x1, matrix products, plane_body(): jnp.einsum('pgqk,pkd->pqgd', probs, v_round.reshape(PLANE, count, HD), pr...  5.73 us

profile of v1, /device:TPU:0, one launch (start us, length us, event | category | flops | bytes accessed | tf_op | source)
XLA Modules:
  0.0 279.9 jit_solution(12563570031631625784)
XLA Ops:
  0.6 4.2 %slice_reduce_fusion.1 = (bf16[320,512]{1,0:T(8,128)(2,1)S(1)}, bf16[320,512]{1,0:T(8,128)(2,1)S(1)}) fusion(bf16[320,2,512]{2,1,0:T(2,128)(2,1)} %param.11), kind=kLoop, calls=%fused_computation.44 | loop fusion | bytes 1310720 | tf_op jit(solution)/shard_map/slice | solution.py:430
  4.8 0.0 copy-start.1
  4.9 0.1 copy_bitcast_fusion.1
  5.0 0.1 copy.54
  5.1 1.3 maximum_bitcast_fusion.w_ref
  6.4 0.7 copy-done.1
  7.2 0.6 fusion.6
  7.8 2.3 fusion.8.x_ref
  10.1 126.0 %shard_map.95 = (bf16[4,2,256,5120]{3,2,1,0:T(8,128)(2,1)}, bf16[4,4,320,640]{3,2,1,0:T(8,128)(2,1)}, s32[4,4,128]{2,1,0:T(4,128)}) custom-call(bf16[256,5120]{1,0:T(8,128)(2,1)} %fusion.8.x_ref, bf16[4,320,640]{2,1,0:T(8,128)(2,1)} %maximum_bitcast_fusion.w_ref, s32[4,128]{1,0:T(4,128)} %bitcast.88), custom_call_target="tpu_custom_call" | custom-call | tf_op jit(solution)/shard_map/pallas_call | solution.py:301
  136.1 20.7 %fusion.26 = f32[2048,640]{1,0:T(8,128)S(1)} fusion(bf16[2048,5120]{1,0:T(8,128)(2,1)} %bitcast.89, bf16[5120,640]{1,0:T(8,128)(2,1)} %bitcast.90), kind=kOutput, calls=%fused_computation.71 | convolution fusion | flops 13421772800 | bytes 32768000 | tf_op jit(solution)/shard_map/dot_general | solution.py:437
  156.8 2.3 copy-done.2
  159.1 1.9 slice.41
  161.0 2.4 copy.30
  163.4 0.3 multiply_reduce_fusion
  163.7 0.3 copy-done.10
  164.0 0.6 multiply_multiply_fusion
  164.6 1.9 slice_negate_fusion
  166.5 3.1 %concatenate.46 = f32[4,512,3,64]{1,0,3,2:T(4,128)} reshape(f32[2048,3,64]{0,2,1:T(8,128)} %get-tuple-element.14) | data formatting | bytes 3145728 | tf_op jit(solution)/shard_map/concatenate | solution.py:24
  169.6 3.1 %concatenate.47 = f32[4,512,3,64]{1,0,3,2:T(4,128)} reshape(f32[2048,3,64]{0,2,1:T(8,128)} %get-tuple-element.15) | data formatting | bytes 3145728 | tf_op jit(solution)/shard_map/concatenate | solution.py:24
  172.8 3.4 %reshape.202 = f32[4,512,3,128]{1,0,3,2:T(4,128)} reshape(f32[2048,384]{0,1:T(8,128)S(1)} %copy.30) | data formatting | bytes 6291456 | tf_op jit(solution)/shard_map/reshape | solution.py:445
  176.2 0.6 convert_reduce_fusion
  176.9 0.1 broadcast_multiply_fusion.1
  177.0 8.4 %fusion.18 = (f32[4,512,128]{1,0,2:T(4,128)S(1)}, f32[4,512,128]{1,0,2:T(4,128)S(1)}) fusion(f32[4,512,64]{1,0,2:T(4,128)S(1)} %broadcast_multiply_fusion.1), kind=kLoop, calls=%fused_computation.41 | loop fusion | flops 262144 | bytes 2621440 | tf_op jit(solution)/shard_map/cos | solution.py:18
  185.4 3.3 %fusion.10 = bf16[4,512,3,128]{1,0,3,2:T(4,128)(2,1)S(1)} fusion(f32[4,512,3,64]{1,0,3,2:T(4,128)} %concatenate.47, f32[4,512,3,64]{1,0,3,2:T(4,128)} %concatenate.46, f32[4,512,3,128]{1,0,3,2:T(4,128)S(1)} %copy-done, f32[4,512,128]{1,0,2:T(4,128)S(1)} %get-tuple-element.19, f32[4,512,128]{1,0,2:T(4,128)S(1)} %get-tuple-element.18, f32[128]{0:T(128)S(1)} %copy-done.10, ...), kind=kLoop, calls=%fused_computation.18 | loop fusion | flops 5505024 | bytes 9986560 | tf_op jit(solution)/shard_map/convert_element_type | solution.py:25
  188.7 0.3 multiply_reduce_fusion.1
  189.1 0.3 fusion.19
  189.5 0.3 fusion.14
  189.8 0.3 broadcast_multiply_fusion
  190.2 5.0 %fusion.16 = bf16[2048,128]{1,0:T(8,128)(2,1)S(1)} fusion(f32[2048,64]{1,0:T(8,128)S(1)} %get-tuple-element.17, f32[2048,64]{1,0:T(8,128)S(1)} %get-tuple-element.16, f32[2048,64]{1,0:T(8,128)S(1)} %broadcast_multiply_fusion, f32[2048,640]{1,0:T(8,128)S(1)} %bitcast.75, f32[128]{0:T(128)S(1)} %copy-done.11, f32[2048]{0:T(1024)S(1)} %add_rsqrt_fusion.1), kind=kLoop, calls=%fused_computation.33 | loop fusion | flops 2097152 | bytes 3154432 | tf_op jit(solution)/shard_map/convert_element_type | solution.py:25
  195.2 1.8 fusion.12
  197.0 0.1 iota_compare_fusion
  197.1 1.7 compare_and_fusion
  198.8 10.9 %fusion.25 = (f32[4,3,512]{2,1,0:T(4,128)S(1)}, f32[4,3,512,512]{2,3,1,0:T(8,128)}) fusion(f32[4,512,512,3]{2,1,3,0:T(8,128)S(1)} %fusion.12, pred[4,512,512]{1,2,0:T(8,128)(4,1)} %compare_and_fusion), kind=kOutput, calls=%fused_computation.70 | output fusion | flops 18874880 | bytes 26238976 | tf_op jit(solution)/shard_map/sub | solution.py:468
  209.7 1.3 slice.58
  211.0 5.7 %fusion.11 = bf16[4,128,3,512]{3,1,2,0:T(8,128)(2,1)S(1)} fusion(bf16[4,512,128,1]{2,1,3,0:T(8,128)(2,1)S(1)} %bitcast.79, f32[4,3,512,512]{2,3,1,0:T(8,128)} %get-tuple-element.23, f32[4,3,512]{2,1,0:T(4,128)S(1)} %get-tuple-element.22), kind=kOutput, calls=%fused_computation.21 | convolution fusion | flops 812384256 | bytes 14704640 | tf_op jit(solution)/shard_map/pgqk,pkd->pqgd/dot_general | solution.py:469
  216.8 0.0 copy-start.8
  216.8 1.6 copy.37.att_ref
  218.3 1.1 pad_maximum_fusion.2.kv_ref
  219.5 0.1 add_select_fusion
  219.5 0.1 copy.35
  219.6 0.1 select_reduce_fusion
  219.7 0.7 copy.36.index_ref
  220.4 3.9 %shard_map.96.page_ref = bf16[16,4,64,256]{3,2,1,0:T(8,128)(2,1)} custom-call(s32[16,4]{1,0:T(8,128)} %copy.36.index_ref, bf16[4,8,64,256]{3,2,1,0:T(8,128)(2,1)} %pad_maximum_fusion.2.kv_ref), custom_call_target="tpu_custom_call" | custom-call | tf_op jit(solution)/shard_map/pallas_call | solution.py:405
  224.2 48.9 %shard_map.97 = (bf16[512,1536]{1,0:T(8,128)(2,1)}, bf16[16,4,64,256]{3,2,1,0:T(8,128)(2,1)}) custom-call(bf16[4,512,384]{2,1,0:T(8,128)(2,1)} %copy.37.att_ref, bf16[16,4,64,256]{3,2,1,0:T(8,128)(2,1)} %shard_map.96.page_ref), custom_call_target="tpu_custom_call" | custom-call | tf_op jit(solution)/shard_map/pallas_call | solution.py:375
  273.1 0.1 compare_reduce_fusion
  273.2 0.6 select_reduce_fusion.1.source_ref
  273.9 4.9 %shard_map.98 = bf16[8,64,2,512]{3,2,1,0:T(2,128)(2,1)} custom-call(s32[8]{0:T(128)} %select_reduce_fusion.1.source_ref, bf16[16,4,64,256]{3,2,1,0:T(8,128)(2,1)} %get-tuple-element.11.in_ref), custom_call_target="tpu_custom_call" | custom-call | tf_op jit(solution)/shard_map/pallas_call | solution.py:494
  278.8 1.1 copy.57
  (33 shorter events, 0.1 us)
Async XLA Ops:
  0.6 4.4 %copy-start.6 = (bf16[320,1536]{1,0:T(8,128)(2,1)S(1)}, bf16[320,1536]{1,0:T(8,128)(2,1)}, u32[]{:S(2)}) copy-start(bf16[320,1536]{1,0:T(8,128)(2,1)} %param.10) | copy-start | bytes 2949124
  4.8 2.3 copy-start.1
  5.1 2.7 copy-start.7
  156.8 2.3 copy-start.2
  163.3 0.7 copy-start.10
  172.8 3.4 %copy-start.9 = (s32[4,4,128]{2,1,0:T(4,128)S(1)}, s32[4,4,128]{2,1,0:T(4,128)}, u32[]{:S(2)}) copy-start(s32[4,4,128]{2,1,0:T(4,128)} %get-tuple-element.9) | copy-start | bytes 24580
  176.2 9.2 %copy-start = (f32[4,512,3,128]{1,0,3,2:T(4,128)S(1)}, f32[4,512,3,128]{1,0,3,2:T(4,128)}, u32[]{:S(2)}) copy-start(f32[4,512,3,128]{1,0,3,2:T(4,128)} %reshape.202) | copy-start | bytes 9437188
  177.0 11.7 %slice-start = ((s8[5242880]{0:T(1024)(128)(4,1)}), s8[4194304]{0:T(1024)(128)(4,1)S(1)}, s32[]{:S(2)}) async-start(s8[5242880]{0:T(1024)(128)(4,1)} %bitcast.74), calls=%async_computation | async-start | bytes 8388608
  185.4 3.3 %slice-start.1 = ((s8[5242880]{0:T(1024)(128)(4,1)}), s8[1048576]{0:T(1024)(128)(4,1)S(1)}, s32[]{:S(2)}) async-start(s8[5242880]{0:T(1024)(128)(4,1)} %bitcast.74), calls=%async_computation.1 | async-start | bytes 2097152
  185.4 3.7 %copy-start.11 = (f32[128]{0:T(128)S(1)}, f32[128]{0:T(128)}, u32[]{:S(2)}) copy-start(f32[128]{0:T(128)} %param.13) | copy-start | bytes 1540
  195.2 1.8 copy-start.3
  216.7 1.6 copy-start.4
  216.8 2.7 copy-start.8
  273.1 5.7 %copy-start.5 = (bf16[512,1536]{1,0:T(8,128)(2,1)S(1)}, bf16[512,1536]{1,0:T(8,128)(2,1)}, u32[]{:S(2)}) copy-start(bf16[512,1536]{1,0:T(8,128)(2,1)} %get-tuple-element.28) | copy-start | bytes 4718596

commit v2 on v1

--- a/solution.py
+++ b/solution.py
@@ -389,25 +389,97 @@
     )(attended, pages)
 
 
-def pick_kernel(index_ref, kv_ref, out_ref):
-    owners, packs = out_ref.shape[0], out_ref.shape[1]
-
-    def one(step, carry):
-        o, p = step // packs, step % packs
-        out_ref[o, p] = kv_ref[p, index_ref[o, p]]
+def attend_kernel(table_ref, x_ref, w_ref, seg_ref, q_gain_ref, k_gain_ref, index_ref, att_ref, out_ref, split, kv):
+    pack = pl.program_id(0)
+    count = seg_ref.shape[2]
+    group = q_gain_ref.shape[0]
+    f32, bf16 = jnp.float32, jnp.bfloat16
+
+    @pl.when(pack == 0)
+    def _():
+        rest = table_ref[...]
+        for i in range(3):
+            part = rest.astype(bf16)
+            split[:, i * HD : (i + 1) * HD] = part
+            rest = rest - part.astype(f32)
+
+    everything = jnp.dot(x_ref[0].reshape(count, -1), w_ref[...], preferred_element_type=f32)
+    row = seg_ref[0]
+    column = jnp.broadcast_to(row.astype(f32), (HD, count)).T[:, :1].astype(jnp.int32)
+    before = jnp.sum((row < column).astype(f32), axis=1, keepdims=True).astype(jnp.int32)
+    i = lax.broadcasted_iota(jnp.int32, (count, count), 0)
+    j = lax.broadcasted_iota(jnp.int32, (count, count), 1)
+    hot = (j == i - before).astype(f32).astype(bf16)
+    allowed = (row == column) & (j <= i)
+    parts = jnp.dot(hot, split[...], preferred_element_type=f32)
+    both = parts[:, :HD] + parts[:, HD : 2 * HD] + parts[:, 2 * HD :]
+    swapped = pltpu.roll(both, HD // 2, 1)
+    low = lax.broadcasted_iota(jnp.int32, (count, HD), 1) < HD // 2
+    cosine = jnp.where(low, both, swapped)
+    sine = jnp.where(low, -swapped, both)
+
+    def turn(values, gain):
+        scaled = values * lax.rsqrt(jnp.mean(values * values, axis=1, keepdims=True) + 1e-06) * gain
+        return (scaled * cosine + pltpu.roll(scaled, HD // 2, 1) * sine).astype(bf16)
+
+    kn = turn(everything[:, group * HD : (group + 1) * HD], k_gain_ref[...])
+    vv = everything[:, (group + 1) * HD :].astype(bf16)
+    pages, page_len = kv.shape[0], kv.shape[1]
+    kv[:, :, :HD] = kn.reshape(pages, page_len, HD)
+    kv[:, :, HD:] = vv.reshape(pages, page_len, HD)
+
+    def one(o, carry):
+        out_ref[o, 0] = kv[index_ref[o, pack]]
         return carry
 
-    lax.fori_loop(0, owners * packs, one, 0)
-
-
-def pick_pages(index, kv):
-    packs, pages, rows, width = kv.shape
+    lax.fori_loop(0, out_ref.shape[0], one, 0)
+    half = count // 2
+    for h in range(group):
+        qn = turn(everything[:, h * HD : (h + 1) * HD], q_gain_ref[h : h + 1])
+        for t in range(2):
+            top, end = t * half, (t + 1) * half
+            scores = lax.dot_general(
+                qn[top:end], kn[:end], (((1,), (1,)), ((), ())), preferred_element_type=f32
+            ) * HD ** (-0.5)
+            scores = jnp.where(allowed[top:end, :end], scores, -1e30)
+            weights = jnp.exp(scores - jnp.max(scores, axis=1, keepdims=True))
+            probs = (weights / jnp.sum(weights, axis=1, keepdims=True)).astype(bf16)
+            att_ref[0, top:end, h * HD : (h + 1) * HD] = jnp.dot(
+                probs, vv[:end], preferred_element_type=f32
+            ).astype(bf16)
+
+
+def attend(table, xs, ws, segs, q_gain, k_gain, index, group, pages):
+    packs, lanes, rows, width = xs.shape
+    count = lanes * rows
+    owners = index.shape[0]
+    page_len = count // pages
+    whole = lambda *shape: pl.BlockSpec(shape, lambda p: (0,) * len(shape))
     return pl.pallas_call(
-        pick_kernel,
-        out_shape=jax.ShapeDtypeStruct((index.shape[0], packs, rows, width), kv.dtype),
-        in_specs=[pl.BlockSpec(memory_space=pltpu.SMEM), pl.BlockSpec(memory_space=pltpu.VMEM)],
-        out_specs=pl.BlockSpec(memory_space=pltpu.VMEM),
-    )(index, kv)
+        attend_kernel,
+        grid=(packs,),
+        out_shape=(
+            jax.ShapeDtypeStruct((packs, count, group * HD), xs.dtype),
+            jax.ShapeDtypeStruct((owners, packs, page_len, 2 * HD), xs.dtype),
+        ),
+        in_specs=[
+            whole(*table.shape),
+            pl.BlockSpec((1, lanes, rows, width), lambda p: (p, 0, 0, 0)),
+            whole(*ws.shape),
+            pl.BlockSpec((1, 1, count), lambda p: (p, 0, 0)),
+            whole(group, HD),
+            whole(1, HD),
+            pl.BlockSpec(memory_space=pltpu.SMEM),
+        ],
+        out_specs=(
+            pl.BlockSpec((1, count, group * HD), lambda p: (p, 0, 0)),
+            pl.BlockSpec((owners, 1, page_len, 2 * HD), lambda p: (0, p, 0, 0)),
+        ),
+        scratch_shapes=[
+            pltpu.VMEM((table.shape[0], 3 * HD), jnp.bfloat16),
+            pltpu.VMEM((pages, page_len, 2 * HD), jnp.bfloat16),
+        ],
+    )(table, xs, ws, segs, jnp.broadcast_to(q_gain[None], (group, HD)), k_gain[None], index)
 
 
 def plane_body(tokens, norm_gain, w_query, w_kv, q_gain, k_gain, seg_ids, page_table):
@@ -433,43 +505,17 @@
         axis=2,
     ).transpose(1, 0, 2)
     count = seg_ids.shape[1]
-    xs, ws, segs = gather(normed, blocks, seg_ids.reshape(-1, HD), depth)
-    everything = jnp.dot(
-        xs.reshape(PLANE * count, -1),
-        ws.reshape(devices * inner, -1),
-        preferred_element_type=jnp.float32,
-    )
-    seg = segs.reshape(PLANE, count)
-    positions = jax.vmap(segment_positions)(seg)
-    cosine, sine = rope_tables(positions.reshape(-1), HD)
-    q_normed = head_norm_rope(everything[:, :q_width].reshape(-1, group, HD), q_gain, cosine, sine)
-    k_normed = head_norm_rope(everything[:, None, q_width : q_width + HD], k_gain, cosine, sine)[:, 0]
-    v_round = everything[:, q_width + HD :].astype(jnp.bfloat16)
     pages_dev = page_table.shape[1]
-    page_len = count // pages_dev
-    kv = jnp.concatenate([k_normed, v_round], axis=1).reshape(PLANE, pages_dev, page_len, 2 * HD)
     rows = lax.dynamic_slice_in_dim(page_table, z * PLANE, PLANE, 0) // pages_dev
     match = rows[None, :, :] == jnp.arange(devices, dtype=jnp.int32)[:, None, None]
     index = jnp.sum(match * jnp.arange(pages_dev, dtype=jnp.int32), axis=2)
-    outgoing = pick_pages(index, kv)
-    scale = HD ** (-0.5)
-    order = jnp.arange(count, dtype=jnp.int32)
-    scores = (
-        jnp.einsum(
-            "pqgd,pkd->pgqk",
-            q_normed.reshape(PLANE, count, group, HD),
-            k_normed.reshape(PLANE, count, HD),
-            preferred_element_type=jnp.float32,
-        )
-        * scale
-    )
-    allowed = (seg[:, :, None] == seg[:, None, :]) & (order[None, None, :] <= order[None, :, None])
-    scores = jnp.where(allowed[:, None], scores, -1e30)
-    probs = jax.nn.softmax(scores, axis=-1).astype(jnp.bfloat16)
-    attended = jnp.einsum(
-        "pgqk,pkd->pqgd", probs, v_round.reshape(PLANE, count, HD), preferred_element_type=jnp.float32
-    )
-    attended = attended.reshape(PLANE, count, q_width).astype(jnp.bfloat16)
+    cosine, sine = rope_tables(jnp.arange(count, dtype=jnp.int32), HD)
+    table = jnp.concatenate([cosine[:, : HD // 2], sine[:, : HD // 2]], axis=1)
+    xs, ws, segs = gather(normed, blocks, seg_ids.reshape(-1, HD), depth)
+    attended, outgoing = attend(
+        table, xs, ws.reshape(devices * inner, -1), segs.reshape(PLANE, 1, count),
+        q_gain, k_gain, index, group, pages_dev,
+    )
     attended, incoming = give_back(attended, outgoing)
     targets = me * pages_dev + jnp.arange(pages_dev, dtype=jnp.int32)
     found = jnp.any(page_table[None, :, :] == targets[:, None, None], axis=2)

time: 281 us -> 237 us (0.84)
  Pallas kernels: 184 us -> 219 us
  other arithmetic: 40.6 us -> 8.8 us
  matrix products: 28.2 us -> 0 us
  local copies, waits for them, and re-layouts: 26.5 us -> 7.74 us
    pallas_call x1, Pallas kernels: 3.86 us -> 39.5 us  [attend(): pl.pallas_call(attend_kernel, grid=(packs,), out_shape=(jax.ShapeDtypeStr...]
    dot_general x3 -> x0, matrix products: 28.2 us -> none  [the longest x1 20.7 us: plane_body(): jnp.dot(xs.reshape(PLANE * count, -1), ws.reshape(devices * inner, -1), p...]
    sub x1 -> x0, other arithmetic: 10.9 us -> none  [plane_body(): probs = jax.nn.softmax(scores, axis=-1).astype(jnp.bfloat16)]
    convert_element_type x2 -> x0, other arithmetic: 8.31 us -> none  [head_norm_rope(): (scaled * cosine[:, None, :] + turned * sine[:, None, :]).astype(jnp.bflo...]
    cos x1, other arithmetic: 8.38 us -> 1.88 us  [rope_tables(): return (jnp.cos(angles), jnp.sin(angles))]
    concatenate x2 -> x0, local copies, waits for them, and re-layouts: 6.28 us -> none  [head_norm_rope(): turned = jnp.concatenate([-scaled[..., half:], scaled[..., :half]], axis=-1)]
    slice x3 -> x0, local copies, waits for them, and re-layouts: 5.52 us -> none  [the longest x2 4.24 us: plane_body(): everything[:, :q_width].reshape(-1, group, HD)]
    reshape x1 -> x0, local copies, waits for them, and re-layouts: 3.41 us -> none  [plane_body(): everything[:, :q_width].reshape(-1, group, HD)]
where the time goes in v2:
time: 237 us
  Pallas kernels  219 us (92%)
  other arithmetic  8.8 us (4%)
  local copies, waits for them, and re-layouts  7.74 us (3%)
    pallas_call x1, Pallas kernels, gather(): pl.pallas_call(functools.partial(gather_kernel, depth), out_shape=(jax.Sh...  126 us
    pallas_call x1, Pallas kernels, give_back(): pl.pallas_call(functools.partial(return_kernel, total), out_shape=(jax.Sh...  48.9 us
    pallas_call x1, Pallas kernels, attend(): pl.pallas_call(attend_kernel, grid=(packs,), out_shape=(jax.ShapeDtypeStr...  39.5 us
    pallas_call x1, Pallas kernels, collect(): pl.pallas_call(collect_kernel, out_shape=jax.ShapeDtypeStruct((slots, row...  4.92 us

profile of v2, /device:TPU:0, one launch (start us, length us, event | category | flops | bytes accessed | tf_op | source)
XLA Modules:
  0.0 236.6 jit_solution(10296712325663752937)
XLA Ops:
  0.6 0.0 copy-start.2
  0.7 0.8 add_select_fusion
  1.5 0.1 copy.20
  1.6 0.1 select_reduce_fusion
  1.7 0.7 copy.21.index_ref
  2.4 4.1 %slice_reduce_fusion.1 = (bf16[320,512]{1,0:T(8,128)(2,1)S(1)}, bf16[320,512]{1,0:T(8,128)(2,1)S(1)}) fusion(bf16[320,2,512]{2,1,0:T(2,128)(2,1)} %param.11), kind=kLoop, calls=%fused_computation.8 | loop fusion | bytes 1310720 | tf_op jit(solution)/shard_map/slice | solution.py:502
  6.5 0.1 copy_bitcast_fusion.1
  6.6 0.0 copy-done.2
  6.6 0.0 copy-start
  6.6 0.1 copy.28
  6.7 0.0 copy-start.3
  6.8 1.3 maximum_bitcast_fusion.w_ref
  8.1 0.9 copy-done
  9.0 0.6 fusion
  9.6 0.0 copy-done.3
  9.6 2.3 fusion.2.x_ref
  11.9 0.0 copy-start.5
  11.9 126.0 %shard_map.95 = (bf16[4,2,256,5120]{3,2,1,0:T(8,128)(2,1)}, bf16[4,4,320,640]{3,2,1,0:T(8,128)(2,1)}, s32[4,4,128]{2,1,0:T(4,128)}) custom-call(bf16[256,5120]{1,0:T(8,128)(2,1)} %fusion.2.x_ref, bf16[4,320,640]{2,1,0:T(8,128)(2,1)} %maximum_bitcast_fusion.w_ref, s32[4,128]{1,0:T(4,128)} %bitcast.26), custom_call_target="tpu_custom_call" | custom-call | tf_op jit(solution)/shard_map/pallas_call | solution.py:301
  137.9 0.1 broadcast_multiply_fusion
  138.1 1.9 maximum_cosine_fusion
  140.0 0.8 pad_maximum_fusion.1.table_ref
  140.8 0.0 copy-done.5
  140.8 0.6 broadcast_in_dim.6.q_gain_ref
  141.4 39.5 %shard_map.96 = (bf16[4,512,384]{2,1,0:T(8,128)(2,1)}, bf16[16,4,64,256]{3,2,1,0:T(8,128)(2,1)}) custom-call(f32[512,128]{1,0:T(8,128)} %pad_maximum_fusion.1.table_ref, bf16[4,2,256,5120]{3,2,1,0:T(8,128)(2,1)} %get-tuple-element.9.x_ref, bf16[5120,640]{1,0:T(8,128)(2,1)} %bitcast.21, s32[4,1,512]{2,1,0:T(1,128)} %bitcast.25, ...), custom_call_target="tpu_custom_call" | custom-call | tf_op jit(solution)/shard_map/pallas_call | solution.py:458
  180.9 0.0 copy-start.4
  180.9 48.9 %shard_map.97 = (bf16[512,1536]{1,0:T(8,128)(2,1)}, bf16[16,4,64,256]{3,2,1,0:T(8,128)(2,1)}) custom-call(bf16[4,512,384]{2,1,0:T(8,128)(2,1)} %get-tuple-element.12.att_ref, bf16[16,4,64,256]{3,2,1,0:T(8,128)(2,1)} %get-tuple-element.13.page_ref), custom_call_target="tpu_custom_call" | custom-call | tf_op jit(solution)/shard_map/pallas_call | solution.py:375
  229.8 0.0 copy-start.1
  229.8 0.0 copy-done.4
  229.8 0.1 compare_reduce_fusion
  229.9 0.6 select_reduce_fusion.1.source_ref
  230.5 4.9 %shard_map.98 = bf16[8,64,2,512]{3,2,1,0:T(2,128)(2,1)} custom-call(s32[8]{0:T(128)} %select_reduce_fusion.1.source_ref, bf16[16,4,64,256]{3,2,1,0:T(8,128)(2,1)} %get-tuple-element.15.in_ref), custom_call_target="tpu_custom_call" | custom-call | tf_op jit(solution)/shard_map/pallas_call | solution.py:540
  235.5 0.0 copy-done.1
  235.5 1.1 copy.30
  (4 shorter events, 0.0 us)
Async XLA Ops:
  0.6 6.0 %copy-start.2 = (bf16[320,1536]{1,0:T(8,128)(2,1)S(1)}, bf16[320,1536]{1,0:T(8,128)(2,1)}, u32[]{:S(2)}) copy-start(bf16[320,1536]{1,0:T(8,128)(2,1)} %param.10) | copy-start | bytes 2949124
  6.6 2.3 copy-start
  6.7 2.8 %copy-start.3 = (f32[5120]{0:T(1024)S(1)}, f32[5120]{0:T(1024)}, u32[]{:S(2)}) copy-start(f32[5120]{0:T(1024)} %param.9) | copy-start | bytes 61444
  11.9 128.9 %copy-start.5 = (f32[128]{0:T(128)S(1)}, f32[128]{0:T(128)}, u32[]{:S(2)}) copy-start(f32[128]{0:T(128)} %param.12) | copy-start | bytes 1540
  180.9 48.9 %copy-start.4 = (s32[16,8]{0,1:T(8,128)S(1)}, s32[16,8]{0,1:T(8,128)}, u32[]{:S(2)}) copy-start(s32[16,8]{0,1:T(8,128)} %param.15) | copy-start | bytes 1540
  229.8 5.7 %copy-start.1 = (bf16[512,1536]{1,0:T(8,128)(2,1)S(1)}, bf16[512,1536]{1,0:T(8,128)(2,1)}, u32[]{:S(2)}) copy-start(bf16[512,1536]{1,0:T(8,128)(2,1)} %get-tuple-element.24) | copy-start | bytes 4718596
